TPU v7x, 32 devices: a whole 2x2x4 slice. The times are simulated.
32 devices in a mesh: tiles: 8 (over z, y), freq: 4 (over x, core).
Axes of the slice: x: 2, y: 2, z: 4, core: 2. Of those that a mesh axis runs over, the one named last changes fastest.
Arguments:
- model_in: bfloat16 [4, 1024, 128], P('freq', 'tiles'), may hold values from -6 to 6
- observed: bfloat16 [4, 1024, 128], P('freq', 'tiles'), may hold values from -6 to 6
- right_factors: bfloat16 [4, 8, 2, 256, 128], P('freq', 'tiles'), may hold values from -0.375 to 0.375
- left_factors: bfloat16 [4, 8, 2, 256, 128], P('freq', 'tiles'), may hold values from -0.25 to 0.25
- tile_map: int32 [8, 2], P('tiles'), may hold values from 0 to 3, as said below
- tile_ranks: int32 [4, 8, 2], P('freq', 'tiles'), may hold values from 1 to 64
- window_mix: float32 [4, 4], replicated, may hold values from 0.1 to 0.6
Outputs:
- residual: float32 [4, 1024, 128], P('freq', 'tiles')
- gradient: float32 [4, 1024, 128], P('freq', 'tiles')
Inputs may be any that keep to these rules, and one draw needn't show every extreme that they name: `tile_map`: devices 2j and 2j+1 of tiles together list every tile row 0 to 3 exactly once, 2 distinct rows each. `tile_ranks`: the rank of the tile named by tile_map in the same slot.
All inputs are finite; a program needn't handle non-finite values.
Results may differ from a plain program's by a relative error of at most 0.0042.
Values may be sent and summed in bfloat16 or wider, within the bound.
A program may use at most 64 MiB of HBM per device.

v0:
```python
import jax
import jax.numpy as jnp
from jax import lax
from jax.sharding import PartitionSpec as P


def from_partner(value, axis, apart):
    mask = 2**apart
    pairs = [(source, source ^ mask) for source in range(lax.axis_size(axis))]
    return lax.ppermute(value, axis, pairs)


def conjugate_apply(factor, values):
    product = jnp.einsum("tar,as->trs", factor, values, preferred_element_type=jnp.float32)
    rank_width = factor.shape[2] // 2
    half_cols = values.shape[1] // 2
    real_part = product[:, :rank_width, :half_cols] + product[:, rank_width:, half_cols:]
    imag_part = product[:, :rank_width, half_cols:] - product[:, rank_width:, :half_cols]
    return jnp.concatenate([real_part, imag_part], axis=2)


def factor_apply(factor, coeffs):
    half_cols = coeffs.shape[2] // 2
    real_part = coeffs[:, :, :half_cols]
    imag_part = coeffs[:, :, half_cols:]
    upper_rows = jnp.concatenate([real_part, imag_part], axis=2)
    lower_rows = jnp.concatenate([-imag_part, real_part], axis=2)
    stacked = jnp.concatenate([upper_rows, lower_rows], axis=1)
    return jnp.einsum("tar,trs->as", factor, stacked, preferred_element_type=jnp.float32)


def rank_mask(ranks, rank_width):
    levels = lax.broadcasted_iota(jnp.int32, (ranks.shape[0], rank_width, 1), 1)
    return levels < ranks[:, None, None]


def ordered(parity, mine, theirs):
    first_order = jnp.concatenate([mine, theirs], axis=0)
    second = jnp.concatenate([theirs, mine], axis=0)
    return jnp.where(parity == 0, first_order, second)


def window_step(mixing, freq_index, rows_pred, rows_data):
    weights_row = lax.dynamic_index_in_dim(mixing, freq_index, 0, keepdims=False)
    weights_col = lax.dynamic_index_in_dim(mixing, freq_index, 1, keepdims=False)
    every_pred = lax.all_gather(rows_pred[None], "freq", axis=0, tiled=True)
    residual_rows = (
        jnp.einsum("g,grs->rs", weights_row, every_pred, precision=lax.Precision.HIGHEST)
        - rows_data
    )
    every_res = lax.all_gather(residual_rows[None], "freq", axis=0, tiled=True)
    adjoint_rows = jnp.einsum("g,grs->rs", weights_col, every_res, precision=lax.Precision.HIGHEST)
    return (residual_rows, adjoint_rows)


def body(model_in, observed, right_factors, left_factors, tile_map, tile_ranks, window_mix):
    tile_index = lax.axis_index("tiles")
    parity = tile_index % 2
    tile_count = lax.axis_size("tiles")
    tile_rows = tile_count // 2
    per_device = tile_map.shape[1]
    freq_index = lax.axis_index("freq")
    right_local = right_factors[0, 0]
    left_local = left_factors[0, 0]
    rank_width = right_local.shape[2] // 2
    half_rows = model_in.shape[1]
    width_cols = model_in.shape[2]
    keep_rows = rank_mask(tile_ranks[0, 0], rank_width)
    column_half = tile_index // 2 // per_device
    own_model = model_in[0]
    other_model = from_partner(own_model, "tiles", 0)
    column_block = ordered(parity, own_model, other_model)
    coeffs = jnp.where(keep_rows, conjugate_apply(right_local, column_block), 0.0).astype(
        jnp.bfloat16
    )
    targets = 2 * tile_map[0] + column_half
    outgoing = jnp.zeros((tile_count, rank_width, width_cols), jnp.bfloat16).at[targets].set(coeffs)
    incoming = lax.all_to_all(outgoing, "tiles", split_axis=0, concat_axis=0, tiled=True)
    paired = incoming.reshape(tile_rows, 2, rank_width, width_cols)
    merged = paired[:, 0] + paired[:, 1]
    row_coeffs = lax.dynamic_slice_in_dim(merged, parity * per_device, per_device, 0)
    partial_value = factor_apply(left_local, row_coeffs)
    own_data = observed[0].astype(jnp.float32)
    given_rows = lax.dynamic_slice_in_dim(partial_value, (1 - parity) * half_rows, half_rows, 0)
    received = from_partner(given_rows, "tiles", 0)
    own_pred = lax.dynamic_slice_in_dim(partial_value, parity * half_rows, half_rows, 0) + received
    residual, own_adjoint = window_step(window_mix, freq_index, own_pred, own_data)
    own_bf = own_adjoint.astype(jnp.bfloat16)
    other_bf = from_partner(own_bf, "tiles", 0)
    adjoint_block = ordered(parity, own_bf, other_bf)
    back_coeffs = conjugate_apply(left_local, adjoint_block).astype(jnp.bfloat16)
    doubled = jnp.repeat(back_coeffs, 2, axis=0)
    empty_slots = jnp.zeros((tile_count, rank_width, width_cols), jnp.bfloat16)
    outgoing_back = lax.dynamic_update_slice_in_dim(
        empty_slots, doubled, parity * 2 * per_device, 0
    )
    returned = lax.all_to_all(outgoing_back, "tiles", split_axis=0, concat_axis=0, tiled=True)
    by_row = lax.dynamic_index_in_dim(
        returned.reshape(tile_rows, 2, rank_width, width_cols), column_half, 1, keepdims=False
    )
    picked = jnp.where(keep_rows, by_row[tile_map[0]], 0.0)
    grad_partial = factor_apply(right_local, picked)
    given_grad = lax.dynamic_slice_in_dim(grad_partial, (1 - parity) * half_rows, half_rows, 0)
    received_grad = from_partner(given_grad, "tiles", 0)
    gradient = (
        lax.dynamic_slice_in_dim(grad_partial, parity * half_rows, half_rows, 0) + received_grad
    )
    return (residual[None], gradient[None])


def solution(mesh):
    placed = (
        P("freq", "tiles", None),
        P("freq", "tiles", None),
        P("freq", "tiles", None, None, None),
        P("freq", "tiles", None, None, None),
        P("tiles", None),
        P("freq", "tiles", None),
        P(),
    )
    return jax.shard_map(
        body,
        mesh=mesh,
        in_specs=placed,
        out_specs=(P("freq", "tiles", None), P("freq", "tiles", None)),
        check_vma=False,
    )
```

profile of v0, /device:TPU:0, one launch (start us, length us, event | category | flops | bytes accessed | tf_op | source)
XLA Modules:
  0.0 64.4 jit_solution(17432492704546929525)
XLA Ops:
  0.6 3.0 %collective-permute-start = (bf16[128,128]{1,0:T(8,128)(2,1)}, bf16[128,128]{1,0:T(8,128)(2,1)S(1)}, u32[]{:S(2)}, u32[]{:S(2)}) collective-permute-start(bf16[128,128]{1,0:T(8,128)(2,1)} %bitcast.89), channel_id=1, source_target_pairs={{0,4},{4,0},{8,12},{12,8},{16,20},{20,16},{24,28},{28,24},{1,5},{5... | collective-permute-start | bytes 98312 | tf_op jit(solution)/shard_map/ppermute | solution.py:10
  3.7 0.7 %copy-done.5 = s32[1,2]{1,0:T(1,128)S(1)} copy-done((s32[1,2]{1,0:T(1,128)S(1)}, s32[1,2]{1,0:T(1,128)}, u32[]{:S(2)}) %copy-start.5) | copy-done | bytes 32
  4.3 0.7 %copy-done.7 = s32[1,1,2]{2,1,0:T(1,128)S(1)} copy-done((s32[1,1,2]{2,1,0:T(1,128)S(1)}, s32[1,1,2]{2,1,0:T(1,128)}, u32[]{:S(2)}) %copy-start.7) | copy-done | bytes 32
  5.1 1.0 %copy.13 = bf16[2,256,128]{1,2,0:T(8,128)(2,1)S(1)} copy(bf16[2,256,128]{2,1,0:T(8,128)(2,1)} %bitcast.82) | data formatting | bytes 262144 | tf_op jit(solution)/shard_map/squeeze | solution.py:63
  6.1 0.2 fusion.4
  6.5 0.7 %broadcast.73.clone = bf16[8,64,128]{2,1,0:T(8,128)(2,1)} broadcast(bf16[]{:T(256)} %constant.63.clone.1), dimensions={} | broadcast | bytes 131074 | tf_op jit(solution)/shard_map/broadcast.8
  7.2 1.9 %scatter_fusion = bf16[8,64,128]{2,1,0:T(8,128)(2,1)} fusion(bf16[8,64,128]{2,1,0:T(8,128)(2,1)} %broadcast.73.clone, s32[2]{0:T(128)S(1)} %get-tuple-element.17, bf16[2,64,128]{2,1,0:T(8,128)(2,1)S(1)} %fusion.10), kind=kCustom, calls=%fused_computation.1 | custom fusion | bytes 98312 | tf_op jit(solution)/shard_map/scatter | solution.py:77
  9.1 6.0 %all-to-all-start = ((bf16[8,64,128]{2,1,0:T(8,128)(2,1)}), bf16[8,64,128]{2,1,0:T(8,128)(2,1)S(1)}, u32[]{:S(2)}, u32[]{:S(2)}) async-start(bf16[8,64,128]{2,1,0:T(8,128)(2,1)} %scatter_fusion), calls=%async_computation | async-start | bytes 262144 | tf_op jit(solution)/shard_map/all_to_all | solution.py:78
  15.1 7.3 %all-to-all-done = bf16[8,64,128]{2,1,0:T(8,128)(2,1)S(1)} async-done(((bf16[8,64,128]{2,1,0:T(8,128)(2,1)}), bf16[8,64,128]{2,1,0:T(8,128)(2,1)S(1)}, u32[]{:S(2)}, u32[]{:S(2)}) %all-to-all-start) | async-done | bytes 131104 | tf_op jit(solution)/shard_map/all_to_all | solution.py:78
  22.6 0.8 %copy-done.1 = bf16[1,1,2,256,128]{4,3,2,1,0:T(8,128)(2,1)S(1)} copy-done((bf16[1,1,2,256,128]{4,3,2,1,0:T(8,128)(2,1)S(1)}, bf16[1,1,2,256,128]{4,3,2,1,0:T(8,128)(2,1)}, u32[]{:S(2)}) %copy-start.1) | copy-done | bytes 131096
  23.4 0.2 convolution_bitcast_fusion.1
  23.6 0.3 collective-permute-start.1
  23.9 0.2 fusion.30
  24.1 3.9 %collective-permute-done.1 = f32[128,128]{0,1:T(8,128)S(1)} collective-permute-done((f32[128,128]{0,1:T(8,128)S(1)}, f32[128,128]{0,1:T(8,128)S(1)}, u32[]{:S(2)}, u32[]{:S(2)}) %collective-permute-start.1) | collective-permute-done | bytes 65568 | tf_op jit(solution)/shard_map/ppermute | solution.py:10
  27.9 5.8 %all-gather = f32[512,128]{0,1:T(8,128)S(1)} all-gather(f32[128,128]{0,1:T(8,128)S(1)} %bitcast_add_fusion.1), channel_id=2, replica_groups=mesh['tiles'=8,'freq'=4] {'freq'}, dimensions={0}, use_global_device_ids=true | all-gather | bytes 327680 | tf_op jit(solution)/shard_map/all_gather | solution.py:46
  33.8 0.6 fusion.32
  34.5 0.7 %copy-done.4 = bf16[1,128,128]{2,1,0:T(8,128)(2,1)S(1)} copy-done((bf16[1,128,128]{2,1,0:T(8,128)(2,1)S(1)}, bf16[1,128,128]{2,1,0:T(8,128)(2,1)}, u32[]{:S(2)}) %copy-start.4) | copy-done | bytes 32792
  35.2 5.9 %all-gather.1 = f32[512,128]{1,0:T(8,128)S(1)} all-gather(f32[128,128]{1,0:T(8,128)S(1)} %convert_subtract_fusion), channel_id=3, replica_groups=mesh['tiles'=8,'freq'=4] {'freq'}, dimensions={0}, use_global_device_ids=true | all-gather | bytes 327680 | tf_op jit(solution)/shard_map/all_gather | solution.py:51
  41.1 0.7 %fusion = f32[1,128,128]{2,0,1:T(1,128)S(1)} fusion(f32[4,128,128]{2,1,0:T(8,128)S(1)} %bitcast.75, f32[4]{0:T(128)S(1)} %fusion.30), kind=kOutput, calls=%fused_computation.4 | convolution fusion | flops 786432 | bytes 327696 | tf_op jit(solution)/shard_map/g,grs->rs/dot_general | solution.py:52
  41.8 0.3 collective-permute-start.2
  42.2 3.6 %collective-permute-done.2 = bf16[128,128]{1,0:T(8,128)(2,1)S(1)} collective-permute-done((bf16[128,128]{1,0:T(8,128)(2,1)S(1)}, bf16[128,128]{1,0:T(8,128)(2,1)S(1)}, u32[]{:S(2)}, u32[]{:S(2)}) %collective-permute-start.2) | collective-permute-done | bytes 32800 | tf_op jit(solution)/shard_map/ppermute | solution.py:10
  45.7 0.2 fusion.16
  46.1 0.7 %broadcast.73 = bf16[8,64,128]{2,1,0:T(8,128)(2,1)} broadcast(bf16[]{:T(256)} %constant.63.clone.1), dimensions={} | broadcast | bytes 131074 | tf_op jit(solution)/shard_map/broadcast.8
  46.8 0.6 constant_dynamic-update-slice_fusion
  47.4 3.4 %all-to-all-start.1 = ((bf16[8,64,128]{2,1,0:T(8,128)(2,1)}), bf16[8,64,128]{2,1,0:T(8,128)(2,1)S(1)}, u32[]{:S(2)}, u32[]{:S(2)}) async-start(bf16[8,64,128]{2,1,0:T(8,128)(2,1)} %constant_dynamic-update-slice_fusion), calls=%async_computation.1 | async-start | bytes 262144 | tf_op jit(solution)/shard_map/all_to_all | solution.py:97
  50.8 7.3 %all-to-all-done.1 = bf16[8,64,128]{2,1,0:T(8,128)(2,1)S(1)} async-done(((bf16[8,64,128]{2,1,0:T(8,128)(2,1)}), bf16[8,64,128]{2,1,0:T(8,128)(2,1)S(1)}, u32[]{:S(2)}, u32[]{:S(2)}) %all-to-all-start.1) | async-done | bytes 131104 | tf_op jit(solution)/shard_map/all_to_all | solution.py:97
  58.1 0.6 gather_fusion
  58.8 0.2 copy-done.2
  59.0 0.3 convolution_bitcast_fusion
  59.3 0.3 collective-permute-start.3
  59.6 4.1 %collective-permute-done.3 = f32[128,128]{0,1:T(8,128)S(1)} collective-permute-done((f32[128,128]{0,1:T(8,128)S(1)}, f32[128,128]{0,1:T(8,128)S(1)}, u32[]{:S(2)}, u32[]{:S(2)}) %collective-permute-start.3) | collective-permute-done | bytes 65568 | tf_op jit(solution)/shard_map/ppermute | solution.py:10
  63.6 0.7 %copy.17 = f32[1,128,128]{2,1,0:T(8,128)} copy(f32[1,128,128]{1,2,0:T(8,128)S(1)} %fusion.27) | data formatting | bytes 131072
  (36 shorter events, 1.2 us)
Async XLA Ops:
  0.6 23.2 %copy-start = (f32[4,4]{1,0:T(4,128)S(1)}, f32[4,4]{1,0:T(4,128)}, u32[]{:S(2)}) copy-start(f32[4,4]{1,0:T(4,128)} %param.13) | copy-start | bytes 196
  0.6 5.4 %collective-permute-start = (bf16[128,128]{1,0:T(8,128)(2,1)}, bf16[128,128]{1,0:T(8,128)(2,1)S(1)}, u32[]{:S(2)}, u32[]{:S(2)}) collective-permute-start(bf16[128,128]{1,0:T(8,128)(2,1)} %bitcast.89), channel_id=1, source_target_pairs={{0,4},{4,0},{8,12},{12,8},{16,20},{20,16},{24,28},{28,24},{1,5},{5... | collective-permute-start | bytes 98312 | tf_op jit(solution)/shard_map/ppermute | solution.py:10
  3.7 0.7 %copy-start.5 = (s32[1,2]{1,0:T(1,128)S(1)}, s32[1,2]{1,0:T(1,128)}, u32[]{:S(2)}) copy-start(s32[1,2]{1,0:T(1,128)} %param.11) | copy-start | bytes 28
  4.3 0.7 %copy-start.7 = (s32[1,1,2]{2,1,0:T(1,128)S(1)}, s32[1,1,2]{2,1,0:T(1,128)}, u32[]{:S(2)}) copy-start(s32[1,1,2]{2,1,0:T(1,128)} %param.12) | copy-start | bytes 28
  5.1 1.0 %copy-start.6 = (bf16[1,128,128]{2,1,0:T(8,128)(2,1)S(1)}, bf16[1,128,128]{2,1,0:T(8,128)(2,1)}, u32[]{:S(2)}) copy-start(bf16[1,128,128]{2,1,0:T(8,128)(2,1)} %param.7) | copy-start | bytes 98308
  9.1 13.4 %all-to-all-start = ((bf16[8,64,128]{2,1,0:T(8,128)(2,1)}), bf16[8,64,128]{2,1,0:T(8,128)(2,1)S(1)}, u32[]{:S(2)}, u32[]{:S(2)}) async-start(bf16[8,64,128]{2,1,0:T(8,128)(2,1)} %scatter_fusion), calls=%async_computation | async-start | bytes 262144 | tf_op jit(solution)/shard_map/all_to_all | solution.py:78
  22.5 0.9 %copy-start.1 = (bf16[1,1,2,256,128]{4,3,2,1,0:T(8,128)(2,1)S(1)}, bf16[1,1,2,256,128]{4,3,2,1,0:T(8,128)(2,1)}, u32[]{:S(2)}) copy-start(bf16[1,1,2,256,128]{4,3,2,1,0:T(8,128)(2,1)} %param.10) | copy-start | bytes 393220
  23.6 4.3 %collective-permute-start.1 = (f32[128,128]{0,1:T(8,128)S(1)}, f32[128,128]{0,1:T(8,128)S(1)}, u32[]{:S(2)}, u32[]{:S(2)}) collective-permute-start(f32[128,128]{0,1:T(8,128)S(1)} %dynamic-slice_bitcast_fusion.2), channel_id=1, source_target_pairs={{0,4},{4,0},{8,12},{12,8},{16,20},{20,16},{24,28},{28,24},{1,5},{5... | collective-permute-start | bytes 196616 | tf_op jit(solution)/shard_map/ppermute | solution.py:10
  34.4 0.8 %copy-start.4 = (bf16[1,128,128]{2,1,0:T(8,128)(2,1)S(1)}, bf16[1,128,128]{2,1,0:T(8,128)(2,1)}, u32[]{:S(2)}) copy-start(bf16[1,128,128]{2,1,0:T(8,128)(2,1)} %param.8) | copy-start | bytes 98308
  35.2 5.9 %copy-start.3 = (f32[128,128]{1,0:T(8,128)}, f32[128,128]{1,0:T(8,128)S(1)}, u32[]{:S(2)}) copy-start(f32[128,128]{1,0:T(8,128)S(1)} %convert_subtract_fusion) | copy-start | bytes 196612
  41.8 4.0 %collective-permute-start.2 = (bf16[128,128]{1,0:T(8,128)(2,1)S(1)}, bf16[128,128]{1,0:T(8,128)(2,1)S(1)}, u32[]{:S(2)}, u32[]{:S(2)}) collective-permute-start(bf16[128,128]{1,0:T(8,128)(2,1)S(1)} %convert_element_type.18), channel_id=1, source_target_pairs={{0,4},{4,0},{8,12},{12,8},{16,20},{20,16},{24,28},{28,24},{1,5},{5... | collective-permute-start | bytes 98312 | tf_op jit(solution)/shard_map/ppermute | solution.py:10
  47.4 10.7 %all-to-all-start.1 = ((bf16[8,64,128]{2,1,0:T(8,128)(2,1)}), bf16[8,64,128]{2,1,0:T(8,128)(2,1)S(1)}, u32[]{:S(2)}, u32[]{:S(2)}) async-start(bf16[8,64,128]{2,1,0:T(8,128)(2,1)} %constant_dynamic-update-slice_fusion), calls=%async_computation.1 | async-start | bytes 262144 | tf_op jit(solution)/shard_map/all_to_all | solution.py:97
  58.1 0.9 %copy-start.2 = (bf16[1,1,2,256,128]{4,3,2,1,0:T(8,128)(2,1)S(1)}, bf16[1,1,2,256,128]{4,3,2,1,0:T(8,128)(2,1)}, u32[]{:S(2)}) copy-start(bf16[1,1,2,256,128]{4,3,2,1,0:T(8,128)(2,1)} %param.9) | copy-start | bytes 393220
  59.3 4.3 %collective-permute-start.3 = (f32[128,128]{0,1:T(8,128)S(1)}, f32[128,128]{0,1:T(8,128)S(1)}, u32[]{:S(2)}, u32[]{:S(2)}) collective-permute-start(f32[128,128]{0,1:T(8,128)S(1)} %dynamic-slice_bitcast_fusion), channel_id=1, source_target_pairs={{0,4},{4,0},{8,12},{12,8},{16,20},{20,16},{24,28},{28,24},{1,5},{5... | collective-permute-start | bytes 196616 | tf_op jit(solution)/shard_map/ppermute | solution.py:10
where the time goes:
time: 65 us; the launch traced here: 64.4 us
  waiting for transfers between devices  26.1 us (40%)
  starting transfers between devices  13.2 us (20%)
  blocking collectives  11.7 us (18%)
  local copies, waits for them, and re-layouts  9.71 us (15%)
  matrix products  2.07 us (3%)
  between operations  0.89 us (1%)
  other arithmetic  0.69 us (1%)
    ppermute x4, waiting for transfers between devices, from_partner(): return lax.ppermute(value, axis, pairs)  11.5 us
    all_to_all x1, waiting for transfers between devices, body(): lax.all_to_all(outgoing, 'tiles', split_axis=0, concat_axis=0, tiled=True)  7.34 us
    all_to_all x1, waiting for transfers between devices, body(): lax.all_to_all(outgoing_back, 'tiles', split_axis=0, concat_axis=0, tiled...  7.26 us
    all_to_all x1, starting transfers between devices, body(): lax.all_to_all(outgoing, 'tiles', split_axis=0, concat_axis=0, tiled=True)  6.01 us
    all_gather x1, blocking collectives, window_step(): every_res = lax.all_gather(residual_rows[None], 'freq', axis=0, tiled=True)  5.86 us
    all_gather x1, blocking collectives, window_step(): every_pred = lax.all_gather(rows_pred[None], 'freq', axis=0, tiled=True)  5.79 us
    ppermute x4, starting transfers between devices, from_partner(): return lax.ppermute(value, axis, pairs)  3.87 us
    unnamed x17, local copies, waits for them, and re-layouts  3.63 us
  transfers between devices with their start and end apart: 6, of which 5 were waited for; matrix products, arithmetic and copies ran while one was open for 2% of the time, Pallas kernels for 0%

commit v1 on v0

v1 whole, which is shorter than its diff:
```python
import functools

import jax
import jax.numpy as jnp
from jax import lax
from jax.experimental import pallas as pl
from jax.experimental.pallas import tpu as pltpu
from jax.sharding import PartitionSpec as P

MESH = pl.DeviceIdType.MESH
F32 = jnp.float32
BF16 = jnp.bfloat16


def each(count, step):
    if count <= 8:
        for k in range(count):
            step(k)
    else:
        lax.fori_loop(0, count, lambda k, carry: (step(k), carry)[1], 0)


def total(count, term, start):
    if count <= 8:
        for k in range(count):
            start = start + term(k)
        return start
    return lax.fori_loop(0, count, lambda k, carry: carry + term(k), start)


def transposed_dot(left, right):
    return lax.dot_general(left, right, (((0,), (0,)), ((), ())), preferred_element_type=F32)


def half_sign(shape):
    lanes = lax.broadcasted_iota(jnp.int32, shape, 1)
    return jnp.where(lanes < shape[1] // 2, 1.0, -1.0).astype(F32)


def conjugate_fold(product):
    rank = product.shape[0] // 2
    low = product[rank:]
    swapped = pltpu.roll(low, low.shape[1] // 2, 1)
    return product[:rank] + half_sign(low.shape) * swapped


def stack_coeffs(coeffs):
    swapped = pltpu.roll(coeffs, coeffs.shape[1] // 2, 1)
    lower = -half_sign(coeffs.shape) * swapped
    return jnp.concatenate([coeffs, lower], axis=0).astype(BF16)


def kernel(
    n_tiles,
    n_freq,
    map_ref,
    rank_ref,
    mix_ref,
    model_ref,
    obs_ref,
    right_ref,
    left_ref,
    res_ref,
    grad_ref,
    x_other,
    obs_all,
    left_other,
    right_masked,
    right_rows,
    right_got,
    coeff_own,
    coeff_send,
    coeff_got,
    stacked,
    pred_send,
    pred_got,
    z_send,
    z_got,
    pair_send,
    pair_recv,
    obs_send,
    obs_recv,
    c_send,
    c_recv,
    p_send,
    p_recv,
    zs_send,
    zs_recv,
):
    tile = lax.axis_index("tiles")
    freq = lax.axis_index("freq")
    parity = lax.rem(tile, 2)
    block = tile // 2
    partner = block * 2 + (1 - parity)
    per_dev = right_ref.shape[2]
    rows = right_ref.shape[3]
    half = rows // 2
    width = right_ref.shape[4]
    rank_width = width // 2
    cols = model_ref.shape[2]
    n_rows = n_tiles // 2

    def tile_at(k):
        return lax.rem(tile + k, n_tiles)

    def freq_at(k):
        return lax.rem(freq + k, n_freq)

    barrier = pltpu.get_barrier_semaphore()

    def greet(k):
        pl.semaphore_signal(
            barrier, inc=1, device_id=(tile_at(k + 1), freq), device_id_type=MESH
        )

    each(n_tiles - 1, greet)
    for k in range(1, n_freq):
        pl.semaphore_signal(barrier, inc=1, device_id=(tile, freq_at(k)), device_id_type=MESH)
    pl.semaphore_wait(barrier, n_tiles - 1 + n_freq - 1)

    def copy(src, dst, send, recv, device):
        return pltpu.make_async_remote_copy(
            src_ref=src,
            dst_ref=dst,
            send_sem=send,
            recv_sem=recv,
            device_id=device,
            device_id_type=MESH,
        )

    own = pl.ds(pl.multiple_of(parity * half, half), half)
    other = pl.ds(pl.multiple_of((1 - parity) * half, half), half)

    x_copy = copy(model_ref.at[0], x_other, pair_send.at[0], pair_recv.at[0], (partner, freq))
    x_copy.start()
    left_copy = copy(
        left_ref.at[0, 0, :, other, :],
        left_other,
        pair_send.at[1],
        pair_recv.at[1],
        (partner, freq),
    )
    left_copy.start()

    def obs_copy(k, source):
        return copy(
            obs_ref.at[0],
            obs_all.at[source],
            obs_send.at[k],
            obs_recv.at[source],
            (tile, freq_at(k)),
        )

    for k in range(1, n_freq):
        obs_copy(k, freq).start()

    lane = lax.rem(lax.broadcasted_iota(jnp.int32, (rows, width), 1), rank_width)

    def mask_right(s):
        keep = lane < rank_ref[0, 0, s]
        right_masked[s] = jnp.where(keep, right_ref[0, 0, s].astype(F32), 0.0).astype(BF16)

    each(per_dev, mask_right)

    x_copy.wait_recv()

    def right_coeffs(s):
        product = transposed_dot(right_masked[s, own, :], model_ref[0]) + transposed_dot(
            right_masked[s, other, :], x_other[...]
        )
        coeff_own[s] = conjugate_fold(product).astype(BF16)

    each(per_dev, right_coeffs)

    def place_coeffs(i):
        def term(s):
            hit = jnp.full((rank_width, cols), map_ref[0, s], jnp.int32) == i
            return jnp.where(hit, coeff_own[s].astype(F32), 0.0)

        coeff_send[i] = total(per_dev, term, jnp.zeros((rank_width, cols), F32)).astype(BF16)

    each(n_rows, place_coeffs)

    def c_copy(k, source):
        target = tile_at(k + 1)
        return copy(
            coeff_send.at[target // 2],
            coeff_got.at[source],
            c_send.at[k],
            c_recv.at[source],
            (target, freq),
        )

    each(n_tiles - 1, lambda k: c_copy(k, tile).start())
    coeff_got[tile] = coeff_send[block]

    def place_right(i):
        def term(rows_at):
            def one(s):
                hit = jnp.full((half, width), map_ref[0, s], jnp.int32) == i
                return jnp.where(hit, right_masked[s, rows_at, :].astype(F32), 0.0)

            return total(per_dev, one, jnp.zeros((half, width), F32)).astype(BF16)

        right_rows[0, i] = term(own)
        right_rows[1, i] = term(other)

    each(n_rows, place_right)
    right_copy = copy(
        right_rows.at[1], right_got, pair_send.at[2], pair_recv.at[2], (partner, freq)
    )

    left_copy.wait_recv()
    each(n_tiles - 1, lambda k: c_copy(k, tile_at(k + 1)).wait_recv())

    def stack_forward(j):
        both = coeff_got[2 * j].astype(F32) + coeff_got[2 * j + 1].astype(F32)
        stacked[j] = stack_coeffs(both)

    each(n_rows, stack_forward)

    def forward_term(s):
        mine = jnp.dot(
            left_ref[0, 0, s, own, :],
            stacked[parity * per_dev + s],
            preferred_element_type=F32,
        )
        theirs = jnp.dot(
            left_other[s], stacked[(1 - parity) * per_dev + s], preferred_element_type=F32
        )
        return mine + theirs

    pred = total(per_dev, forward_term, jnp.zeros((half, cols), F32))
    pred_send[...] = pred.astype(BF16)

    def p_copy(k, source):
        return copy(
            pred_send,
            pred_got.at[source],
            p_send.at[k],
            p_recv.at[source],
            (tile, freq_at(k)),
        )

    for k in range(1, n_freq):
        p_copy(k, freq).start()
    right_copy.start()

    res = mix_ref[freq, freq] * pred - obs_ref[0].astype(F32)

    def gram(at):
        weight = mix_ref[0, freq] * mix_ref[0, at]
        for g in range(1, n_freq):
            weight = weight + mix_ref[g, freq] * mix_ref[g, at]
        return weight

    adjoint = gram(freq) * pred - mix_ref[freq, freq] * obs_ref[0].astype(F32)
    for k in range(1, n_freq):
        source = freq_at(k)
        obs_copy(k, source).wait_recv()
        adjoint = adjoint - mix_ref[source, freq] * obs_all[source].astype(F32)
    for k in range(1, n_freq):
        source = freq_at(k)
        p_copy(k, source).wait_recv()
        got = pred_got[source].astype(F32)
        res = res + mix_ref[freq, source] * got
        adjoint = adjoint + gram(source) * got
    adjoint_bf = adjoint.astype(BF16)

    def back(s):
        mine = transposed_dot(left_ref[0, 0, s, own, :], adjoint_bf)
        z_send[parity * per_dev + s] = conjugate_fold(mine).astype(BF16)
        theirs = transposed_dot(left_other[s], adjoint_bf)
        z_send[(1 - parity) * per_dev + s] = conjugate_fold(theirs).astype(BF16)

    each(per_dev, back)

    def z_copy(k, source):
        target = tile_at(k + 1)
        return copy(
            z_send.at[target // 2],
            z_got.at[source],
            zs_send.at[k],
            zs_recv.at[source],
            (target, freq),
        )

    each(n_tiles - 1, lambda k: z_copy(k, tile).start())
    z_got[tile] = z_send[block]
    res_ref[0] = res

    right_copy.wait_recv()

    def merge_right(i):
        right_rows[0, i] = (right_rows[0, i].astype(F32) + right_got[i].astype(F32)).astype(BF16)

    each(n_rows, merge_right)
    each(n_tiles - 1, lambda k: z_copy(k, tile_at(k + 1)).wait_recv())

    def gradient_term(i):
        both = z_got[2 * i].astype(F32) + z_got[2 * i + 1].astype(F32)
        return jnp.dot(right_rows[0, i], stack_coeffs(both), preferred_element_type=F32)

    grad_ref[0] = total(n_rows, gradient_term, jnp.zeros((half, cols), F32))

    x_copy.wait_send()
    left_copy.wait_send()
    right_copy.wait_send()
    for k in range(1, n_freq):
        obs_copy(k, freq).wait_send()
        p_copy(k, freq).wait_send()
    each(n_tiles - 1, lambda k: c_copy(k, tile).wait_send())
    each(n_tiles - 1, lambda k: z_copy(k, tile).wait_send())


def body(model_in, observed, right_factors, left_factors, tile_map, tile_ranks, window_mix):
    n_tiles = lax.axis_size("tiles")
    n_freq = lax.axis_size("freq")
    n_rows = n_tiles // 2
    per_dev, rows, width = right_factors.shape[2:]
    half = rows // 2
    cols = model_in.shape[2]
    rank = width // 2
    vmem = pl.BlockSpec(memory_space=pltpu.VMEM)
    smem = pl.BlockSpec(memory_space=pltpu.SMEM)
    dma = pltpu.SemaphoreType.DMA
    field = jax.ShapeDtypeStruct((1, half, cols), F32)
    return pl.pallas_call(
        functools.partial(kernel, n_tiles, n_freq),
        out_shape=(field, field),
        in_specs=[smem, smem, smem, vmem, vmem, vmem, vmem],
        out_specs=(vmem, vmem),
        scratch_shapes=[
            pltpu.VMEM((half, cols), BF16),
            pltpu.VMEM((n_freq, half, cols), BF16),
            pltpu.VMEM((per_dev, half, width), BF16),
            pltpu.VMEM((per_dev, rows, width), BF16),
            pltpu.VMEM((2, n_rows, half, width), BF16),
            pltpu.VMEM((n_rows, half, width), BF16),
            pltpu.VMEM((per_dev, rank, cols), BF16),
            pltpu.VMEM((n_rows, rank, cols), BF16),
            pltpu.VMEM((n_tiles, rank, cols), BF16),
            pltpu.VMEM((n_rows, width, cols), BF16),
            pltpu.VMEM((half, cols), BF16),
            pltpu.VMEM((n_freq, half, cols), BF16),
            pltpu.VMEM((n_rows, rank, cols), BF16),
            pltpu.VMEM((n_tiles, rank, cols), BF16),
            dma((3,)),
            dma((3,)),
            dma((n_freq,)),
            dma((n_freq,)),
            dma((n_tiles,)),
            dma((n_tiles,)),
            dma((n_freq,)),
            dma((n_freq,)),
            dma((n_tiles,)),
            dma((n_tiles,)),
        ],
        compiler_params=pltpu.CompilerParams(
            collective_id=0, has_side_effects=True, vmem_limit_bytes=40 * 1024 * 1024
        ),
        name="deconvolve",
    )(tile_map, tile_ranks, window_mix, model_in, observed, right_factors, left_factors)


def solution(mesh):
    placed = (
        P("freq", "tiles", None),
        P("freq", "tiles", None),
        P("freq", "tiles", None, None, None),
        P("freq", "tiles", None, None, None),
        P("tiles", None),
        P("freq", "tiles", None),
        P(),
    )
    return jax.shard_map(
        body,
        mesh=mesh,
        in_specs=placed,
        out_specs=(P("freq", "tiles", None), P("freq", "tiles", None)),
        check_vma=False,
    )
```

time: 65 us -> 31 us (0.48)
  waiting for transfers between devices: 26.1 us -> 0 us
  Pallas kernels: 0 us -> 23.5 us
  starting transfers between devices: 13.2 us -> 0 us
  blocking collectives: 11.7 us -> 0 us
  local copies, waits for them, and re-layouts: 9.71 us -> 6.57 us
  matrix products: 2.07 us -> 0 us
  other arithmetic: 0.69 us -> 0 us
    pallas_call x0 -> x1, Pallas kernels: none -> 23.5 us  [body(): pl.pallas_call(functools.partial(kernel, n_tiles, n_freq), out_shape=(fie...]
    all_to_all x2 -> x0, waiting for transfers between devices: 14.6 us -> none  [the longest x1 7.34 us: body(): lax.all_to_all(outgoing, 'tiles', split_axis=0, concat_axis=0, tiled=True)]
    all_gather x2 -> x0, blocking collectives: 11.7 us -> none  [the longest x1 5.86 us: window_step(): every_res = lax.all_gather(residual_rows[None], 'freq', axis=0, tiled=True)]
    ppermute x4 -> x0, waiting for transfers between devices: 11.5 us -> none  [from_partner(): return lax.ppermute(value, axis, pairs)]
    all_to_all x2 -> x0, starting transfers between devices: 9.38 us -> none  [the longest x1 6.01 us: body(): lax.all_to_all(outgoing, 'tiles', split_axis=0, concat_axis=0, tiled=True)]
    ppermute x4 -> x0, starting transfers between devices: 3.87 us -> none  [from_partner(): return lax.ppermute(value, axis, pairs)]
    unnamed x17 -> x16, local copies, waits for them, and re-layouts: 3.63 us -> 6.57 us
    scatter x1 -> x0, local copies, waits for them, and re-layouts: 1.89 us -> none  [body(): jnp.zeros((tile_count, rank_width, width_cols), jnp.bfloat16).at[targets]]
  transfers between devices with their start and end apart: 6 -> 0, of which waited for: 5 -> 0; matrix products, arithmetic and copies ran while one was open for 2% -> 0% of each run, Pallas kernels for 0% -> 0%
where the time goes in v1:
time: 31 us; the launch traced here: 30.7 us
  Pallas kernels  23.5 us (76%)
  local copies, waits for them, and re-layouts  6.57 us (21%)
  between operations  0.66 us (2%)
    pallas_call x1, Pallas kernels, body(): pl.pallas_call(functools.partial(kernel, n_tiles, n_freq), out_shape=(fie...  23.5 us
    unnamed x16, local copies, waits for them, and re-layouts  6.57 us

profile of v1, /device:TPU:0, one launch (start us, length us, event | category | flops | bytes accessed | tf_op | source)
XLA Modules:
  0.0 30.7 jit_solution(14077931579245445903)
XLA Ops:
  0.6 0.0 copy-start
  0.6 0.9 %copy-done = bf16[1,1,2,256,128]{4,3,2,1,0:T(8,128)(2,1)S(1)} copy-done((bf16[1,1,2,256,128]{4,3,2,1,0:T(8,128)(2,1)S(1)}, bf16[1,1,2,256,128]{4,3,2,1,0:T(8,128)(2,1)}, u32[]{:S(2)}) %copy-start) | copy-done | bytes 131096
  1.5 0.0 copy-start.1
  1.5 0.9 %copy-done.1 = bf16[1,1,2,256,128]{4,3,2,1,0:T(8,128)(2,1)S(1)} copy-done((bf16[1,1,2,256,128]{4,3,2,1,0:T(8,128)(2,1)S(1)}, bf16[1,1,2,256,128]{4,3,2,1,0:T(8,128)(2,1)}, u32[]{:S(2)}) %copy-start.1) | copy-done | bytes 131096
  2.4 0.0 copy-start.2
  2.4 0.8 %copy-done.2 = bf16[1,128,128]{2,1,0:T(8,128)(2,1)S(1)} copy-done((bf16[1,128,128]{2,1,0:T(8,128)(2,1)S(1)}, bf16[1,128,128]{2,1,0:T(8,128)(2,1)}, u32[]{:S(2)}) %copy-start.2) | copy-done | bytes 32792
  3.2 0.0 copy-start.3
  3.2 0.8 %copy-done.3 = bf16[1,128,128]{2,1,0:T(8,128)(2,1)S(1)} copy-done((bf16[1,128,128]{2,1,0:T(8,128)(2,1)S(1)}, bf16[1,128,128]{2,1,0:T(8,128)(2,1)}, u32[]{:S(2)}) %copy-start.3) | copy-done | bytes 32792
  4.0 0.0 copy-start.4
  4.0 0.7 %copy-done.4 = f32[4,4]{1,0:T(4,128)S(1)} copy-done((f32[4,4]{1,0:T(4,128)S(1)}, f32[4,4]{1,0:T(4,128)}, u32[]{:S(2)}) %copy-start.4) | copy-done | bytes 88
  4.6 0.0 copy-start.5
  4.6 0.7 %copy-done.5 = s32[1,2]{1,0:T(1,128)S(1)} copy-done((s32[1,2]{1,0:T(1,128)S(1)}, s32[1,2]{1,0:T(1,128)}, u32[]{:S(2)}) %copy-start.5) | copy-done | bytes 32
  5.3 0.0 copy-start.6
  5.3 0.7 %copy-done.6 = s32[1,1,2]{2,1,0:T(1,128)S(1)} copy-done((s32[1,1,2]{2,1,0:T(1,128)S(1)}, s32[1,1,2]{2,1,0:T(1,128)}, u32[]{:S(2)}) %copy-start.6) | copy-done | bytes 32
  6.0 23.5 %deconvolve.1 = (f32[1,128,128]{2,1,0:T(8,128)S(1)}, f32[1,128,128]{2,1,0:T(8,128)S(1)}) custom-call(s32[1,2]{1,0:T(1,128)S(1)} %copy-done.5, s32[1,1,2]{2,1,0:T(1,128)S(1)} %copy-done.6, f32[4,4]{1,0:T(4,128)S(1)} %copy-done.4, bf16[1,128,128]{2,1,0:T(8,128)(2,1)S(1)} %copy-done.2, bf16[1,128,128]{2,1,0:T(8,128)(2,1)S(1)} %copy-done.3, ...), custom_call_target="tpu_custom_call" | custom-call | tf_op jit(solution)/shard_map/deconvolve/pallas_call | solution.py:328
  29.4 0.6 %copy.11 = f32[1,128,128]{2,1,0:T(8,128)} copy(f32[1,128,128]{2,1,0:T(8,128)S(1)} %get-tuple-element.4) | data formatting | bytes 131072
  30.1 0.6 %copy.12 = f32[1,128,128]{2,1,0:T(8,128)} copy(f32[1,128,128]{2,1,0:T(8,128)S(1)} %get-tuple-element.5) | data formatting | bytes 131072
Async XLA Ops:
  0.6 0.9 %copy-start = (bf16[1,1,2,256,128]{4,3,2,1,0:T(8,128)(2,1)S(1)}, bf16[1,1,2,256,128]{4,3,2,1,0:T(8,128)(2,1)}, u32[]{:S(2)}) copy-start(bf16[1,1,2,256,128]{4,3,2,1,0:T(8,128)(2,1)} %right_ref.1) | copy-start | bytes 393220
  1.5 0.9 %copy-start.1 = (bf16[1,1,2,256,128]{4,3,2,1,0:T(8,128)(2,1)S(1)}, bf16[1,1,2,256,128]{4,3,2,1,0:T(8,128)(2,1)}, u32[]{:S(2)}) copy-start(bf16[1,1,2,256,128]{4,3,2,1,0:T(8,128)(2,1)} %left_ref.1) | copy-start | bytes 393220
  2.4 0.8 %copy-start.2 = (bf16[1,128,128]{2,1,0:T(8,128)(2,1)S(1)}, bf16[1,128,128]{2,1,0:T(8,128)(2,1)}, u32[]{:S(2)}) copy-start(bf16[1,128,128]{2,1,0:T(8,128)(2,1)} %model_ref.1) | copy-start | bytes 98308
  3.2 0.8 %copy-start.3 = (bf16[1,128,128]{2,1,0:T(8,128)(2,1)S(1)}, bf16[1,128,128]{2,1,0:T(8,128)(2,1)}, u32[]{:S(2)}) copy-start(bf16[1,128,128]{2,1,0:T(8,128)(2,1)} %obs_ref.1) | copy-start | bytes 98308
  4.0 0.7 %copy-start.4 = (f32[4,4]{1,0:T(4,128)S(1)}, f32[4,4]{1,0:T(4,128)}, u32[]{:S(2)}) copy-start(f32[4,4]{1,0:T(4,128)} %mix_ref.1) | copy-start | bytes 196
  4.6 0.7 %copy-start.5 = (s32[1,2]{1,0:T(1,128)S(1)}, s32[1,2]{1,0:T(1,128)}, u32[]{:S(2)}) copy-start(s32[1,2]{1,0:T(1,128)} %map_ref.1) | copy-start | bytes 28
  5.3 0.7 %copy-start.6 = (s32[1,1,2]{2,1,0:T(1,128)S(1)}, s32[1,1,2]{2,1,0:T(1,128)}, u32[]{:S(2)}) copy-start(s32[1,1,2]{2,1,0:T(1,128)} %rank_ref.1) | copy-start | bytes 28

commit v2 on v1

--- a/solution.py
+++ b/solution.py
@@ -53,6 +53,15 @@
 def kernel(
     n_tiles,
     n_freq,
+    map_hbm,
+    rank_hbm,
+    mix_hbm,
+    model_hbm,
+    obs_hbm,
+    right_hbm,
+    left_hbm,
+    res_ref,
+    grad_ref,
     map_ref,
     rank_ref,
     mix_ref,
@@ -60,8 +69,7 @@
     obs_ref,
     right_ref,
     left_ref,
-    res_ref,
-    grad_ref,
+    in_sem,
     x_other,
     obs_all,
     left_other,
@@ -106,6 +114,20 @@
     def freq_at(k):
         return lax.rem(freq + k, n_freq)
 
+    inputs = [
+        pltpu.make_async_copy(src, dst, in_sem.at[at])
+        for at, (src, dst) in enumerate(
+            [
+                (right_hbm, right_ref),
+                (rank_hbm, rank_ref),
+                (model_hbm, model_ref),
+                (map_hbm, map_ref),
+                (left_hbm, left_ref),
+                (obs_hbm, obs_ref),
+                (mix_hbm, mix_ref),
+            ]
+        )
+    ]
     barrier = pltpu.get_barrier_semaphore()
 
     def greet(k):
@@ -116,6 +138,17 @@
     each(n_tiles - 1, greet)
     for k in range(1, n_freq):
         pl.semaphore_signal(barrier, inc=1, device_id=(tile, freq_at(k)), device_id_type=MESH)
+    for one in inputs:
+        one.start()
+    inputs[0].wait()
+    inputs[1].wait()
+    lane = lax.rem(lax.broadcasted_iota(jnp.int32, (rows, width), 1), rank_width)
+
+    def mask_right(s):
+        keep = lane < rank_ref[0, 0, s]
+        right_masked[s] = jnp.where(keep, right_ref[0, 0, s].astype(F32), 0.0).astype(BF16)
+
+    each(per_dev, mask_right)
     pl.semaphore_wait(barrier, n_tiles - 1 + n_freq - 1)
 
     def copy(src, dst, send, recv, device):
@@ -131,10 +164,10 @@
     own = pl.ds(pl.multiple_of(parity * half, half), half)
     other = pl.ds(pl.multiple_of((1 - parity) * half, half), half)
 
-    x_copy = copy(model_ref.at[0], x_other, pair_send.at[0], pair_recv.at[0], (partner, freq))
+    x_copy = copy(model_hbm.at[0], x_other, pair_send.at[0], pair_recv.at[0], (partner, freq))
     x_copy.start()
     left_copy = copy(
-        left_ref.at[0, 0, :, other, :],
+        left_hbm.at[0, 0, :, other, :],
         left_other,
         pair_send.at[1],
         pair_recv.at[1],
@@ -144,7 +177,7 @@
 
     def obs_copy(k, source):
         return copy(
-            obs_ref.at[0],
+            obs_hbm.at[0],
             obs_all.at[source],
             obs_send.at[k],
             obs_recv.at[source],
@@ -154,14 +187,8 @@
     for k in range(1, n_freq):
         obs_copy(k, freq).start()
 
-    lane = lax.rem(lax.broadcasted_iota(jnp.int32, (rows, width), 1), rank_width)
-
-    def mask_right(s):
-        keep = lane < rank_ref[0, 0, s]
-        right_masked[s] = jnp.where(keep, right_ref[0, 0, s].astype(F32), 0.0).astype(BF16)
-
-    each(per_dev, mask_right)
-
+    inputs[2].wait()
+    inputs[3].wait()
     x_copy.wait_recv()
 
     def right_coeffs(s):
@@ -210,6 +237,8 @@
         right_rows.at[1], right_got, pair_send.at[2], pair_recv.at[2], (partner, freq)
     )
 
+    for one in inputs[4:]:
+        one.wait()
     left_copy.wait_recv()
     each(n_tiles - 1, lambda k: c_copy(k, tile_at(k + 1)).wait_recv())
 
@@ -322,15 +351,23 @@
     cols = model_in.shape[2]
     rank = width // 2
     vmem = pl.BlockSpec(memory_space=pltpu.VMEM)
-    smem = pl.BlockSpec(memory_space=pltpu.SMEM)
+    hbm = pl.BlockSpec(memory_space=pl.ANY)
     dma = pltpu.SemaphoreType.DMA
     field = jax.ShapeDtypeStruct((1, half, cols), F32)
     return pl.pallas_call(
         functools.partial(kernel, n_tiles, n_freq),
         out_shape=(field, field),
-        in_specs=[smem, smem, smem, vmem, vmem, vmem, vmem],
+        in_specs=[hbm] * 7,
         out_specs=(vmem, vmem),
         scratch_shapes=[
+            pltpu.SMEM(tile_map.shape, jnp.int32),
+            pltpu.SMEM(tile_ranks.shape, jnp.int32),
+            pltpu.SMEM(window_mix.shape, F32),
+            pltpu.VMEM(model_in.shape, BF16),
+            pltpu.VMEM(observed.shape, BF16),
+            pltpu.VMEM(right_factors.shape, BF16),
+            pltpu.VMEM(left_factors.shape, BF16),
+            dma((7,)),
             pltpu.VMEM((half, cols), BF16),
             pltpu.VMEM((n_freq, half, cols), BF16),
             pltpu.VMEM((per_dev, half, width), BF16),
@@ -357,7 +394,7 @@
             dma((n_tiles,)),
         ],
         compiler_params=pltpu.CompilerParams(
-            collective_id=0, has_side_effects=True, vmem_limit_bytes=40 * 1024 * 1024
+            collective_id=0, has_side_effects=True, vmem_limit_bytes=62 * 1024 * 1024
         ),
         name="deconvolve",
     )(tile_map, tile_ranks, window_mix, model_in, observed, right_factors, left_factors)

time: 31 us -> 26.8 us (0.86)
  local copies, waits for them, and re-layouts: 6.57 us -> 2.14 us
    unnamed x16 -> x4, local copies, waits for them, and re-layouts: 6.57 us -> 2.14 us
    pallas_call x1, Pallas kernels: 23.5 us -> 23.8 us  [body(): pl.pallas_call(functools.partial(kernel, n_tiles, n_freq), out_shape=(fie...]
where the time goes in v2:
time: 26.8 us; the launch traced here: 26.6 us
  Pallas kernels  23.8 us (89%)
  local copies, waits for them, and re-layouts  2.14 us (8%)
  between operations  0.65 us (2%)
    pallas_call x1, Pallas kernels, body(): pl.pallas_call(functools.partial(kernel, n_tiles, n_freq), out_shape=(fie...  23.8 us
    unnamed x4, local copies, waits for them, and re-layouts  2.14 us

profile of v2, /device:TPU:0, one launch (start us, length us, event | category | flops | bytes accessed | tf_op | source)
XLA Modules:
  0.0 26.6 jit_solution(7379342426623374714)
XLA Ops:
  0.6 23.8 %deconvolve.1 = (f32[1,128,128]{2,1,0:T(8,128)}, f32[1,128,128]{2,1,0:T(8,128)}) custom-call(s32[1,2]{1,0:T(1,128)} %map_hbm.1, s32[1,1,2]{2,1,0:T(1,128)} %rank_hbm.1, f32[4,4]{1,0:T(4,128)} %mix_hbm.1, bf16[1,128,128]{2,1,0:T(8,128)(2,1)} %model_hbm.1, bf16[1,128,128]{2,1,0:T(8,128)(2,1)} %obs_hbm.1, bf16[1,1,2,256,128]{4,3,2,1,0:T(8,128)(2,1)} %right_hbm.1, ...), custom_call_target="tpu_custom_call" | custom-call | tf_op jit(solution)/shard_map/deconvolve/pallas_call | solution.py:357
  24.4 0.0 copy-start
  24.5 1.5 %copy.11 = f32[1,128,128]{2,1,0:T(8,128)} copy(f32[1,128,128]{2,1,0:T(8,128)} %get-tuple-element.4) | data formatting | bytes 131072
  26.0 0.0 copy-done
  26.0 0.6 %copy.12 = f32[1,128,128]{2,1,0:T(8,128)} copy(f32[1,128,128]{2,1,0:T(8,128)S(1)} %copy-done) | data formatting | bytes 131072
Async XLA Ops:
  24.4 1.5 %copy-start = (f32[1,128,128]{2,1,0:T(8,128)S(1)}, f32[1,128,128]{2,1,0:T(8,128)}, u32[]{:S(2)}) copy-start(f32[1,128,128]{2,1,0:T(8,128)} %get-tuple-element.5) | copy-start | bytes 196612

commit v3 on v2

--- a/solution.py
+++ b/solution.py
@@ -394,10 +394,10 @@
             dma((n_tiles,)),
         ],
         compiler_params=pltpu.CompilerParams(
-            collective_id=0, has_side_effects=True, vmem_limit_bytes=62 * 1024 * 1024
+            collective_id=0, has_side_effects=True, vmem_limit_bytes=40 * 1024 * 1024
         ),
         name="deconvolve",
-    )(tile_map, tile_ranks, window_mix, model_in, observed, right_factors, left_factors)
+    )(*[pltpu.with_memory_space_constraint(a, pltpu.HBM) for a in (tile_map, tile_ranks, window_mix, model_in, observed, right_factors, left_factors)])
 
 
 def solution(mesh):

time: 26.8 us -> 25.2 us (0.940)
  local copies, waits for them, and re-layouts: 2.14 us -> 1.26 us
  Pallas kernels: 23.8 us -> 23.2 us
    unnamed x4 -> x2, local copies, waits for them, and re-layouts: 2.14 us -> 1.26 us
    pallas_call x1, Pallas kernels: 23.8 us -> 23.2 us  [body(): pl.pallas_call(functools.partial(kernel, n_tiles, n_freq), out_shape=(fie...]
where the time goes in v3:
time: 25.2 us; the launch traced here: 25.1 us
  Pallas kernels  23.2 us (92%)
  local copies, waits for them, and re-layouts  1.26 us (5%)
  between operations  0.64 us (3%)
    pallas_call x1, Pallas kernels, body(): pl.pallas_call(functools.partial(kernel, n_tiles, n_freq), out_shape=(fie...  23.2 us
    unnamed x2, local copies, waits for them, and re-layouts  1.26 us

profile of v3, /device:TPU:0, one launch (start us, length us, event | category | flops | bytes accessed | tf_op | source)
XLA Modules:
  0.0 25.1 jit_solution(1859815684749627679)
XLA Ops:
  0.6 23.2 %deconvolve.1 = (f32[1,128,128]{2,1,0:T(8,128)S(1)}, f32[1,128,128]{2,1,0:T(8,128)S(1)}) custom-call(s32[1,2]{1,0:T(1,128)} %map_hbm.1, s32[1,1,2]{2,1,0:T(1,128)} %rank_hbm.1, f32[4,4]{1,0:T(4,128)} %mix_hbm.1, bf16[1,128,128]{2,1,0:T(8,128)(2,1)} %model_hbm.1, bf16[1,128,128]{2,1,0:T(8,128)(2,1)} %obs_hbm.1, bf16[1,1,2,256,128]{4,3,2,1,0:T(8,128)(2,1)} %right_hbm.1, ...), custom_call_target="tpu_custom_call" | custom-call | tf_op jit(solution)/shard_map/deconvolve/pallas_call | solution.py:357
  23.8 0.6 %copy.11 = f32[1,128,128]{2,1,0:T(8,128)} copy(f32[1,128,128]{2,1,0:T(8,128)S(1)} %get-tuple-element.4) | data formatting | bytes 131072
  24.4 0.6 %copy.12 = f32[1,128,128]{2,1,0:T(8,128)} copy(f32[1,128,128]{2,1,0:T(8,128)S(1)} %get-tuple-element.5) | data formatting | bytes 131072

commit v4 on v3

--- a/solution.py
+++ b/solution.py
@@ -68,18 +68,16 @@
     model_ref,
     obs_ref,
     right_ref,
-    left_ref,
+    left_rows,
     in_sem,
     x_other,
     obs_all,
-    left_other,
     right_masked,
     right_rows,
     right_got,
     coeff_own,
     coeff_send,
     coeff_got,
-    stacked,
     pred_send,
     pred_got,
     z_send,
@@ -114,6 +112,18 @@
     def freq_at(k):
         return lax.rem(freq + k, n_freq)
 
+    def row_far(k):
+        upper = block // (n_rows // 2)
+        first = (1 - upper) * (n_rows - 1 - k) + upper * k
+        down = (block - first + n_rows) // n_rows
+        up = (first - block + n_rows) // n_rows
+        return first - (1 - upper) * down + upper * up
+
+    freq_order = sorted(range(1, n_freq), key=lambda k: abs(k - n_freq // 2))
+
+    own = pl.ds(pl.multiple_of(parity * half, half), half)
+    other = pl.ds(pl.multiple_of((1 - parity) * half, half), half)
+    own_slots = pl.ds(parity * per_dev, per_dev)
     inputs = [
         pltpu.make_async_copy(src, dst, in_sem.at[at])
         for at, (src, dst) in enumerate(
@@ -122,7 +132,7 @@
                 (rank_hbm, rank_ref),
                 (model_hbm, model_ref),
                 (map_hbm, map_ref),
-                (left_hbm, left_ref),
+                (left_hbm.at[0, 0, :, own, :], left_rows.at[own_slots]),
                 (obs_hbm, obs_ref),
                 (mix_hbm, mix_ref),
             ]
@@ -161,14 +171,11 @@
             device_id_type=MESH,
         )
 
-    own = pl.ds(pl.multiple_of(parity * half, half), half)
-    other = pl.ds(pl.multiple_of((1 - parity) * half, half), half)
-
     x_copy = copy(model_hbm.at[0], x_other, pair_send.at[0], pair_recv.at[0], (partner, freq))
     x_copy.start()
     left_copy = copy(
         left_hbm.at[0, 0, :, other, :],
-        left_other,
+        left_rows.at[own_slots],
         pair_send.at[1],
         pair_recv.at[1],
         (partner, freq),
@@ -206,19 +213,23 @@
 
         coeff_send[i] = total(per_dev, term, jnp.zeros((rank_width, cols), F32)).astype(BF16)
 
-    each(n_rows, place_coeffs)
-
-    def c_copy(k, source):
-        target = tile_at(k + 1)
+    def c_copy(target, source):
         return copy(
             coeff_send.at[target // 2],
             coeff_got.at[source],
-            c_send.at[k],
+            c_send.at[target],
             c_recv.at[source],
             (target, freq),
         )
 
-    each(n_tiles - 1, lambda k: c_copy(k, tile).start())
+    def c_start(k):
+        place_coeffs(row_far(k))
+        c_copy(2 * row_far(k), tile).start()
+        c_copy(2 * row_far(k) + 1, tile).start()
+
+    each(n_rows - 1, c_start)
+    place_coeffs(block)
+    c_copy(partner, tile).start()
     coeff_got[tile] = coeff_send[block]
 
     def place_right(i):
@@ -240,26 +251,20 @@
     for one in inputs[4:]:
         one.wait()
     left_copy.wait_recv()
-    each(n_tiles - 1, lambda k: c_copy(k, tile_at(k + 1)).wait_recv())
-
-    def stack_forward(j):
+    def forward_term(j):
         both = coeff_got[2 * j].astype(F32) + coeff_got[2 * j + 1].astype(F32)
-        stacked[j] = stack_coeffs(both)
-
-    each(n_rows, stack_forward)
-
-    def forward_term(s):
-        mine = jnp.dot(
-            left_ref[0, 0, s, own, :],
-            stacked[parity * per_dev + s],
-            preferred_element_type=F32,
-        )
-        theirs = jnp.dot(
-            left_other[s], stacked[(1 - parity) * per_dev + s], preferred_element_type=F32
-        )
-        return mine + theirs
-
-    pred = total(per_dev, forward_term, jnp.zeros((half, cols), F32))
+        return jnp.dot(left_rows[j], stack_coeffs(both), preferred_element_type=F32)
+
+    c_copy(partner, partner).wait_recv()
+    pred = forward_term(block)
+
+    def forward_near(k):
+        j = row_far(n_rows - 2 - k)
+        c_copy(2 * j, 2 * j).wait_recv()
+        c_copy(2 * j + 1, 2 * j + 1).wait_recv()
+        return forward_term(j)
+
+    pred = total(n_rows - 1, forward_near, pred)
     pred_send[...] = pred.astype(BF16)
 
     def p_copy(k, source):
@@ -271,7 +276,7 @@
             (tile, freq_at(k)),
         )
 
-    for k in range(1, n_freq):
+    for k in freq_order:
         p_copy(k, freq).start()
     right_copy.start()
 
@@ -296,25 +301,28 @@
         adjoint = adjoint + gram(source) * got
     adjoint_bf = adjoint.astype(BF16)
 
-    def back(s):
-        mine = transposed_dot(left_ref[0, 0, s, own, :], adjoint_bf)
-        z_send[parity * per_dev + s] = conjugate_fold(mine).astype(BF16)
-        theirs = transposed_dot(left_other[s], adjoint_bf)
-        z_send[(1 - parity) * per_dev + s] = conjugate_fold(theirs).astype(BF16)
-
-    each(per_dev, back)
-
-    def z_copy(k, source):
-        target = tile_at(k + 1)
+    def back(j):
+        product = transposed_dot(left_rows[j], adjoint_bf)
+        z_send[j] = conjugate_fold(product).astype(BF16)
+
+    def z_copy(target, source):
         return copy(
             z_send.at[target // 2],
             z_got.at[source],
-            zs_send.at[k],
+            zs_send.at[target],
             zs_recv.at[source],
             (target, freq),
         )
 
-    each(n_tiles - 1, lambda k: z_copy(k, tile).start())
+    def z_start(k):
+        j = row_far(k)
+        back(j)
+        z_copy(2 * j, tile).start()
+        z_copy(2 * j + 1, tile).start()
+
+    each(n_rows - 1, z_start)
+    back(block)
+    z_copy(partner, tile).start()
     z_got[tile] = z_send[block]
     res_ref[0] = res
 
@@ -324,13 +332,20 @@
         right_rows[0, i] = (right_rows[0, i].astype(F32) + right_got[i].astype(F32)).astype(BF16)
 
     each(n_rows, merge_right)
-    each(n_tiles - 1, lambda k: z_copy(k, tile_at(k + 1)).wait_recv())
-
     def gradient_term(i):
         both = z_got[2 * i].astype(F32) + z_got[2 * i + 1].astype(F32)
         return jnp.dot(right_rows[0, i], stack_coeffs(both), preferred_element_type=F32)
 
-    grad_ref[0] = total(n_rows, gradient_term, jnp.zeros((half, cols), F32))
+    z_copy(partner, partner).wait_recv()
+    grad = gradient_term(block)
+
+    def gradient_near(k):
+        i = row_far(n_rows - 2 - k)
+        z_copy(2 * i, 2 * i).wait_recv()
+        z_copy(2 * i + 1, 2 * i + 1).wait_recv()
+        return gradient_term(i)
+
+    grad_ref[0] = total(n_rows - 1, gradient_near, grad)
 
     x_copy.wait_send()
     left_copy.wait_send()
@@ -338,8 +353,8 @@
     for k in range(1, n_freq):
         obs_copy(k, freq).wait_send()
         p_copy(k, freq).wait_send()
-    each(n_tiles - 1, lambda k: c_copy(k, tile).wait_send())
-    each(n_tiles - 1, lambda k: z_copy(k, tile).wait_send())
+    each(n_tiles - 1, lambda k: c_copy(tile_at(k + 1), tile).wait_send())
+    each(n_tiles - 1, lambda k: z_copy(tile_at(k + 1), tile).wait_send())
 
 
 def body(model_in, observed, right_factors, left_factors, tile_map, tile_ranks, window_mix):
@@ -366,18 +381,16 @@
             pltpu.VMEM(model_in.shape, BF16),
             pltpu.VMEM(observed.shape, BF16),
             pltpu.VMEM(right_factors.shape, BF16),
-            pltpu.VMEM(left_factors.shape, BF16),
+            pltpu.VMEM((n_rows, half, width), BF16),
             dma((7,)),
             pltpu.VMEM((half, cols), BF16),
             pltpu.VMEM((n_freq, half, cols), BF16),
-            pltpu.VMEM((per_dev, half, width), BF16),
             pltpu.VMEM((per_dev, rows, width), BF16),
             pltpu.VMEM((2, n_rows, half, width), BF16),
             pltpu.VMEM((n_rows, half, width), BF16),
             pltpu.VMEM((per_dev, rank, cols), BF16),
             pltpu.VMEM((n_rows, rank, cols), BF16),
             pltpu.VMEM((n_tiles, rank, cols), BF16),
-            pltpu.VMEM((n_rows, width, cols), BF16),
             pltpu.VMEM((half, cols), BF16),
             pltpu.VMEM((n_freq, half, cols), BF16),
             pltpu.VMEM((n_rows, rank, cols), BF16),

time: 25.2 us -> 25 us (level)
  Pallas kernels: 23.2 us -> 22.9 us
where the time goes in v4:
time: 25 us; the launch traced here: 24.8 us
  Pallas kernels  22.9 us (92%)
  local copies, waits for them, and re-layouts  1.26 us (5%)
  between operations  0.64 us (3%)
    pallas_call x1, Pallas kernels, body(): pl.pallas_call(functools.partial(kernel, n_tiles, n_freq), out_shape=(fie...  22.9 us
    unnamed x2, local copies, waits for them, and re-layouts  1.26 us

profile of v4, /device:TPU:0, one launch (start us, length us, event | category | flops | bytes accessed | tf_op | source)
XLA Modules:
  0.0 24.8 jit_solution(5258520424535679802)
XLA Ops:
  0.6 22.9 %deconvolve.1 = (f32[1,128,128]{2,1,0:T(8,128)S(1)}, f32[1,128,128]{2,1,0:T(8,128)S(1)}) custom-call(s32[1,2]{1,0:T(1,128)} %map_hbm.1, s32[1,1,2]{2,1,0:T(1,128)} %rank_hbm.1, f32[4,4]{1,0:T(4,128)} %mix_hbm.1, bf16[1,128,128]{2,1,0:T(8,128)(2,1)} %model_hbm.1, bf16[1,128,128]{2,1,0:T(8,128)(2,1)} %obs_hbm.1, bf16[1,1,2,256,128]{4,3,2,1,0:T(8,128)(2,1)} %right_hbm.1, ...), custom_call_target="tpu_custom_call" | custom-call | tf_op jit(solution)/shard_map/deconvolve/pallas_call | solution.py:372
  23.6 0.6 %copy.11 = f32[1,128,128]{2,1,0:T(8,128)} copy(f32[1,128,128]{2,1,0:T(8,128)S(1)} %get-tuple-element.4) | data formatting | bytes 131072
  24.2 0.6 %copy.12 = f32[1,128,128]{2,1,0:T(8,128)} copy(f32[1,128,128]{2,1,0:T(8,128)S(1)} %get-tuple-element.5) | data formatting | bytes 131072

commit v5 on v4

--- a/solution.py
+++ b/solution.py
@@ -357,6 +357,17 @@
     each(n_tiles - 1, lambda k: z_copy(tile_at(k + 1), tile).wait_send())
 
 
+def write_out(res_in, grad_in, res_out, grad_out, sem):
+    copies = [
+        pltpu.make_async_copy(res_in, res_out, sem.at[0]),
+        pltpu.make_async_copy(grad_in, grad_out, sem.at[1]),
+    ]
+    for one in copies:
+        one.start()
+    for one in copies:
+        one.wait()
+
+
 def body(model_in, observed, right_factors, left_factors, tile_map, tile_ranks, window_mix):
     n_tiles = lax.axis_size("tiles")
     n_freq = lax.axis_size("freq")
@@ -369,7 +380,7 @@
     hbm = pl.BlockSpec(memory_space=pl.ANY)
     dma = pltpu.SemaphoreType.DMA
     field = jax.ShapeDtypeStruct((1, half, cols), F32)
-    return pl.pallas_call(
+    results = pl.pallas_call(
         functools.partial(kernel, n_tiles, n_freq),
         out_shape=(field, field),
         in_specs=[hbm] * 7,
@@ -411,6 +422,14 @@
         ),
         name="deconvolve",
     )(*[pltpu.with_memory_space_constraint(a, pltpu.HBM) for a in (tile_map, tile_ranks, window_mix, model_in, observed, right_factors, left_factors)])
+    return pl.pallas_call(
+        write_out,
+        out_shape=(field, field),
+        in_specs=[vmem, vmem],
+        out_specs=(hbm, hbm),
+        scratch_shapes=[dma((2,))],
+        name="write_out",
+    )(*[pltpu.with_memory_space_constraint(a, pltpu.VMEM) for a in results])
 
 
 def solution(mesh):

time: 25 us -> 24.4 us (0.976)
  local copies, waits for them, and re-layouts: 1.26 us -> 0 us
  Pallas kernels: 22.9 us -> 23.6 us
    unnamed x2 -> x0, local copies, waits for them, and re-layouts: 1.26 us -> none
    pallas_call x0 -> x1, Pallas kernels: none -> 0.67 us  [body(): pl.pallas_call(write_out, out_shape=(field, field), in_specs=[vmem, vmem]...]
where the time goes in v5:
time: 24.4 us; the launch traced here: 24.2 us
  Pallas kernels  23.6 us (97%)
  between operations  0.64 us (3%)
    pallas_call x1, Pallas kernels, body(): pl.pallas_call(functools.partial(kernel, n_tiles, n_freq), out_shape=(fie...  22.9 us
    pallas_call x1, Pallas kernels, body(): pl.pallas_call(write_out, out_shape=(field, field), in_specs=[vmem, vmem]...  0.67 us

profile of v5, /device:TPU:0, one launch (start us, length us, event | category | flops | bytes accessed | tf_op | source)
XLA Modules:
  0.0 24.2 jit_solution(17941993743992690077)
XLA Ops:
  0.6 22.9 %deconvolve.1 = (f32[1,128,128]{2,1,0:T(8,128)S(1)}, f32[1,128,128]{2,1,0:T(8,128)S(1)}) custom-call(s32[1,2]{1,0:T(1,128)} %map_hbm.1, s32[1,1,2]{2,1,0:T(1,128)} %rank_hbm.1, f32[4,4]{1,0:T(4,128)} %mix_hbm.1, bf16[1,128,128]{2,1,0:T(8,128)(2,1)} %model_hbm.1, bf16[1,128,128]{2,1,0:T(8,128)(2,1)} %obs_hbm.1, bf16[1,1,2,256,128]{4,3,2,1,0:T(8,128)(2,1)} %right_hbm.1, ...), custom_call_target="tpu_custom_call" | custom-call | tf_op jit(solution)/shard_map/deconvolve/pallas_call | solution.py:383
  23.6 0.7 %write_out.1 = (f32[1,128,128]{2,1,0:T(8,128)}, f32[1,128,128]{2,1,0:T(8,128)}) custom-call(f32[1,128,128]{2,1,0:T(8,128)S(1)} %get-tuple-element.4.res_in, f32[1,128,128]{2,1,0:T(8,128)S(1)} %get-tuple-element.5.grad_in), custom_call_target="tpu_custom_call" | custom-call | tf_op jit(solution)/shard_map/write_out/pallas_call | solution.py:425
